TPU v7x, 32 devices: a whole 2x2x4 slice. The times are simulated.
32 devices in a mesh: lat: 4 (over y, core), lon: 8 (over z, x).
Axes of the slice: x: 2, y: 2, z: 4, core: 2. Of those that a mesh axis runs over, the one named last changes fastest.
Arguments:
- tracers: bfloat16 [10, 4, 64, 1024], P(None, None, 'lat', 'lon'), may hold values from -6 to 6
- winds: float32 [3, 4, 64, 1024], P(None, None, 'lat', 'lon'), may hold values from -2.5 to 2.5
- zonal_shift: int32 [64], P('lat'), may hold values from 0 to 1023
Outputs:
- new_tracers: bfloat16 [10, 4, 64, 1024], P(None, None, 'lat', 'lon')
- displacement: float32 [3, 4, 64, 1024], P(None, None, 'lat', 'lon')
All inputs are finite; a program needn't handle non-finite values.
Results may differ from a plain program's by a relative error of at most 0.001.
Values may be sent and summed in bfloat16 or wider, within the bound.
A program may use at most 64 MiB of HBM per device.

v0:
```python
import jax
import jax.numpy as jnp
from jax import lax
from jax.sharding import PartitionSpec as P

ITERS = 3
RIM = 4


def shifted_2(x, axis, by):
    length = lax.axis_size(axis)
    return lax.ppermute(x, axis, [(i, (i + by) % length) for i in range(length)])


def padded(block, sides, width):
    for axis, dim in sides:
        count = lax.axis_size(axis)
        forward = [(i, i + 1) for i in range(count - 1)]
        forward.append((count - 1, 0))
        backward = [(target, source) for source, target in forward]
        low = lax.ppermute(
            lax.slice_in_dim(block, block.shape[dim] - width, None, axis=dim), axis, forward
        )
        high = lax.ppermute(lax.slice_in_dim(block, 0, width, axis=dim), axis, backward)
        block = jnp.concatenate([low, block, high], axis=dim)
    return block


def cubic_weights(frac):
    return (
        -frac * (frac - 1.0) * (frac - 2.0) / 6.0,
        (frac + 1.0) * (frac - 1.0) * (frac - 2.0) / 2.0,
        -(frac + 1.0) * frac * (frac - 2.0) / 2.0,
        (frac + 1.0) * frac * (frac - 1.0) / 6.0,
    )


def spread(base, weights, lowest, highest):
    listed = []
    for target in range(lowest, highest + 1):
        summed = jnp.zeros(base.shape, jnp.float32)
        for a in range(len(weights)):
            summed = summed + jnp.where(base + a == target, weights[a], 0.0)
        listed.append(summed)
    return listed


def pole_zero(block, width, anchor, total_rows):
    rowpos = lax.broadcasted_iota(jnp.int32, (block.shape[2], 1), 0) + anchor - width
    keep = (rowpos >= 0) & (rowpos < total_rows)
    return jnp.where(keep, block, jnp.zeros_like(block))


def translate_doubling(block, shifts):
    cols = block.shape[3]
    sectors = shifts // cols
    within = shifts - sectors * cols
    steps = (lax.axis_size("lon") - 1).bit_length()
    for bit in range(steps):
        moved = shifted_2(block, "lon", 1 << bit)
        chosen = (sectors >> bit & 1 == 1)[:, None]
        block = jnp.where(chosen, moved, block)
    western = shifted_2(block, "lon", 1)
    joined = jnp.concatenate([western, block], axis=3)
    offset = cols - within
    for bit in range(cols.bit_length()):
        step_cols = 1 << bit
        padding = jnp.zeros(joined.shape[:3] + (step_cols,), joined.dtype)
        shifted = jnp.concatenate([joined[:, :, :, step_cols:], padding], axis=3)
        chosen = (offset >> bit & 1 == 1)[:, None]
        joined = jnp.where(chosen, shifted, joined)
    return joined[:, :, :, :cols]


def local(tracers, winds, zonal_shift):
    ntrac, levels, rows, cols = tracers.shape
    total_rows = rows * lax.axis_size("lat")
    anchor = lax.axis_index("lat") * rows
    shape = (levels, rows, cols)
    kpos = lax.broadcasted_iota(jnp.float32, shape, 0)
    kint = lax.broadcasted_iota(jnp.int32, shape, 0)
    growi = lax.broadcasted_iota(jnp.int32, shape, 1) + anchor
    gpos = growi.astype(jnp.float32)
    wide = padded(winds, (("lat", 2), ("lon", 3)), 2)
    wide = pole_zero(wide, 2, anchor, total_rows)
    wide = jnp.pad(wide, ((0, 0), (2, 2), (0, 0), (0, 0)))
    disp = winds
    for step in range(ITERS):
        zlev = jnp.clip(kpos - 0.5 * disp[0], 0.0, levels - 1.0)
        ylat = jnp.clip(gpos - 0.5 * disp[1], 0.0, total_rows - 1.0)
        wind_xrel = -0.5 * disp[2]
        wind_zb = jnp.floor(zlev)
        wind_yb = jnp.floor(ylat)
        wind_xb = jnp.floor(wind_xrel)
        tz = zlev - wind_zb
        ty = ylat - wind_yb
        tx = wind_xrel - wind_xb
        wind_z_weights = spread(wind_zb.astype(jnp.int32) - kint, (1.0 - tz, tz), -2, 2)
        wind_y_weights = spread(wind_yb.astype(jnp.int32) - growi, (1.0 - ty, ty), -2, 2)
        wind_x_weights = spread(wind_xb.astype(jnp.int32), (1.0 - tx, tx), -2, 2)
        total = jnp.zeros((3,) + shape, jnp.float32)
        for wind_iz in range(5):
            wind_plane = jnp.zeros((3,) + shape, jnp.float32)
            for wind_iy in range(5):
                wind_line = jnp.zeros((3,) + shape, jnp.float32)
                for wind_ix in range(5):
                    wind_line = (
                        wind_line
                        + wind_x_weights[wind_ix]
                        * wide[
                            :,
                            wind_iz : wind_iz + levels,
                            wind_iy : wind_iy + rows,
                            wind_ix : wind_ix + cols,
                        ]
                    )
                wind_plane = wind_plane + wind_y_weights[wind_iy] * wind_line
            total = total + wind_z_weights[wind_iz] * wind_plane
        disp = total
    moved = translate_doubling(tracers, zonal_shift)
    source = padded(moved, (("lat", 2), ("lon", 3)), RIM)
    source = pole_zero(source, RIM, anchor, total_rows)
    source = jnp.pad(source, ((0, 0), (4, 4), (0, 0), (0, 0)))
    lanes = []
    for oy in range(-4, 5):
        lanes.append(source[:, :, RIM + oy : RIM + oy + rows, RIM - 4 : RIM + cols + 4])
    zdep = jnp.clip(kpos - disp[0], 0.0, levels - 1.0)
    ydep = jnp.clip(gpos - disp[1], 0.0, total_rows - 1.0)
    xrel = -disp[2]
    zb = jnp.floor(zdep)
    yb = jnp.floor(ydep)
    xb = jnp.floor(xrel)
    z_weights = spread(zb.astype(jnp.int32) - kint - 1, cubic_weights(zdep - zb), -4, 4)
    y_weights = spread(yb.astype(jnp.int32) - growi - 1, cubic_weights(ydep - yb), -4, 4)
    x_weights = spread(xb.astype(jnp.int32) - 1, cubic_weights(xrel - xb), -4, 4)
    result = jnp.zeros((ntrac,) + shape, jnp.float32)
    for iz in range(9):
        plane = jnp.zeros((ntrac,) + shape, jnp.float32)
        for iy in range(9):
            line = jnp.zeros((ntrac,) + shape, jnp.float32)
            for ix in range(9):
                line = line + x_weights[ix] * lanes[iy][:, iz : iz + levels, :, ix : ix + cols]
            plane = plane + y_weights[iy] * line
        result = result + z_weights[iz] * plane
    return (result.astype(jnp.bfloat16), disp)


def solution(mesh):
    return jax.shard_map(
        local,
        mesh=mesh,
        in_specs=(P(None, None, "lat", "lon"), P(None, None, "lat", "lon"), P("lat")),
        out_specs=(P(None, None, "lat", "lon"), P(None, None, "lat", "lon")),
        check_vma=False,
    )
```

profile of v0, /device:TPU:0, one launch (start us, length us, event | category | flops | bytes accessed | tf_op | source)
XLA Modules:
  0.0 113.8 jit_solution(14658361860781212974)
XLA Ops:
  0.6 0.9 fusion.45
  1.5 0.5 collective-permute-start
  2.1 2.0 %collective-permute-start.1 = (f32[3,4,2,128]{3,2,1,0:T(2,128)S(1)}, f32[3,4,2,128]{3,2,1,0:T(2,128)S(1)}, u32[]{:S(2)}, u32[]{:S(2)}) collective-permute-start(f32[3,4,2,128]{3,2,1,0:T(2,128)S(1)} %get-tuple-element.99), channel_id=1, source_target_pairs={{8,0},{16,8},{24,16},{0,24},{9,1},{17,9},{25,17},{1,25},{10,2},{18... | collective-permute-start | bytes 36872 | tf_op jit(solution)/shard_map/ppermute | solution.py:24
  4.1 2.2 %collective-permute-start.4 = (bf16[10,4,16,128]{3,2,1,0:T(8,128)(2,1)}, bf16[10,4,16,128]{3,2,1,0:T(8,128)(2,1)S(1)}, u32[]{:S(2)}, u32[]{:S(2)}) collective-permute-start(bf16[10,4,16,128]{3,2,1,0:T(8,128)(2,1)} %param.3), channel_id=1, source_target_pairs={{0,1},{1,2},{2,3},{3,4},{4,5},{5,6},{6,7},{7,0},{8,9},{9,10},{10,1... | collective-permute-start | bytes 491528 | tf_op jit(solution)/shard_map/ppermute | solution.py:12
  6.3 0.7 and_compare_fusion.10
  7.0 0.9 add_bitcast_fusion.69
  8.1 1.6 %collective-permute-start.2 = (f32[3,4,20,2]{3,2,1,0:T(8,128)S(1)}, f32[3,4,20,2]{3,2,1,0:T(8,128)S(1)}, u32[]{:S(2)}, u32[]{:S(2)}) collective-permute-start(f32[3,4,20,2]{3,2,1,0:T(8,128)S(1)} %get-tuple-element.20), channel_id=1, source_target_pairs={{0,1},{1,2},{2,3},{3,4},{4,5},{5,6},{6,7},{7,0},{8,9},{9,10},{10,1... | collective-permute-start | bytes 5768 | tf_op jit(solution)/shard_map/ppermute | solution.py:21
  9.7 3.2 %collective-permute-start.3 = (f32[3,4,20,2]{3,2,1,0:T(8,128)S(1)}, f32[3,4,20,2]{3,2,1,0:T(8,128)S(1)}, u32[]{:S(2)}, u32[]{:S(2)}) collective-permute-start(f32[3,4,20,2]{3,2,1,0:T(8,128)S(1)} %get-tuple-element.21), channel_id=1, source_target_pairs={{1,0},{2,1},{3,2},{4,3},{5,4},{6,5},{7,6},{0,7},{9,8},{10,9},{11,1... | collective-permute-start | bytes 5768 | tf_op jit(solution)/shard_map/ppermute | solution.py:24
  12.9 4.2 %collective-permute-done.2 = f32[3,4,20,2]{3,2,1,0:T(8,128)S(1)} collective-permute-done((f32[3,4,20,2]{3,2,1,0:T(8,128)S(1)}, f32[3,4,20,2]{3,2,1,0:T(8,128)S(1)}, u32[]{:S(2)}, u32[]{:S(2)}) %collective-permute-start.2) | collective-permute-done | bytes 1952 | tf_op jit(solution)/shard_map/ppermute | solution.py:21
  17.0 3.1 %collective-permute-done.3 = f32[3,4,20,2]{3,2,1,0:T(8,128)S(1)} collective-permute-done((f32[3,4,20,2]{3,2,1,0:T(8,128)S(1)}, f32[3,4,20,2]{3,2,1,0:T(8,128)S(1)}, u32[]{:S(2)}, u32[]{:S(2)}) %collective-permute-start.3) | collective-permute-done | bytes 1952 | tf_op jit(solution)/shard_map/ppermute | solution.py:24
  20.1 0.2 maximum_select_fusion.1
  20.4 1.8 %multiply_add_fusion.6 = f32[3,4,16,128]{3,2,1,0:T(8,128)S(1)} fusion(f32[3,4,20,132]{3,2,1,0:T(8,128)S(1)} %maximum_select_fusion.1, f32[4,16,128]{2,1,0:T(8,128)S(1)} %get-tuple-element.90, f32[4,16,128]{2,1,0:T(8,128)S(1)} %get-tuple-element.86, f32[4,16,128]{2,1,0:T(8,128)S(1)} %get-tuple-element.85, f32[4,16,128]{2,1,0:T(8,128)S(1)} %get-tuple-element.84, ...), kind=kLoop, calls=%fused_computation.616 | loop fusion | flops 6856704 | bytes 3342336 | tf_op jit(solution)/shard_map/add | solution.py:118
  22.3 1.8 %multiply_add_fusion.5 = f32[3,4,16,128]{3,2,1,0:T(8,128)S(1)} fusion(f32[3,4,20,132]{3,2,1,0:T(8,128)S(1)} %maximum_select_fusion.1, f32[4,16,128]{2,1,0:T(8,128)S(1)} %get-tuple-element.75, f32[4,16,128]{2,1,0:T(8,128)S(1)} %get-tuple-element.71, f32[4,16,128]{2,1,0:T(8,128)S(1)} %get-tuple-element.70, f32[4,16,128]{2,1,0:T(8,128)S(1)} %get-tuple-element.69, ...), kind=kLoop, calls=%fused_computation.615 | loop fusion | flops 6856704 | bytes 3342336 | tf_op jit(solution)/shard_map/add | solution.py:118
  24.5 7.8 %collective-permute-done.5 = bf16[10,4,16,128]{3,2,1,0:T(8,128)(2,1)S(1)} collective-permute-done((bf16[10,4,16,128]{3,2,1,0:T(8,128)(2,1)S(1)}, bf16[10,4,16,128]{3,2,1,0:T(8,128)(2,1)S(1)}, u32[]{:S(2)}, u32[]{:S(2)}) %collective-permute-start.5) | collective-permute-done | bytes 163872 | tf_op jit(solution)/shard_map/ppermute | solution.py:12
  32.4 1.8 %multiply_add_fusion.4 = f32[3,4,16,128]{3,2,1,0:T(8,128)S(1)} fusion(f32[3,4,20,132]{3,2,1,0:T(8,128)S(1)} %maximum_select_fusion.1, f32[4,16,128]{2,1,0:T(8,128)S(1)} %get-tuple-element.60, f32[4,16,128]{2,1,0:T(8,128)S(1)} %get-tuple-element.56, f32[4,16,128]{2,1,0:T(8,128)S(1)} %get-tuple-element.55, f32[4,16,128]{2,1,0:T(8,128)S(1)} %get-tuple-element.54, ...), kind=kLoop, calls=%fused_computation.614 | loop fusion | flops 6856704 | bytes 3342336 | tf_op jit(solution)/shard_map/add | solution.py:118
  34.3 6.0 %collective-permute-done.6 = bf16[10,4,16,128]{3,2,1,0:T(8,128)(2,1)S(1)} collective-permute-done((bf16[10,4,16,128]{3,2,1,0:T(8,128)(2,1)S(1)}, bf16[10,4,16,128]{3,2,1,0:T(8,128)(2,1)S(1)}, u32[]{:S(2)}, u32[]{:S(2)}) %collective-permute-start.6) | collective-permute-done | bytes 163872 | tf_op jit(solution)/shard_map/ppermute | solution.py:12
  40.5 0.3 add_bitcast_fusion.2
  40.7 8.5 %collective-permute-done.7 = bf16[10,4,16,128]{3,2,1,0:T(8,128)(2,1)S(1)} collective-permute-done((bf16[10,4,16,128]{3,2,1,0:T(8,128)(2,1)S(1)}, bf16[10,4,16,128]{3,2,1,0:T(8,128)(2,1)S(1)}, u32[]{:S(2)}, u32[]{:S(2)}) %collective-permute-start.7) | collective-permute-done | bytes 163872 | tf_op jit(solution)/shard_map/ppermute | solution.py:12
  49.3 0.2 fusion
  49.5 0.2 fusion.1
  49.7 0.2 slice.4183
  50.0 0.2 slice.4184
  50.3 0.2 slice.4185
  51.7 0.2 pad_select_fusion
  52.0 1.7 %collective-permute-start.9 = (bf16[10,4,4,128]{3,2,1,0:T(4,128)(2,1)S(1)}, bf16[10,4,4,128]{3,2,1,0:T(4,128)(2,1)S(1)}, u32[]{:S(2)}, u32[]{:S(2)}) collective-permute-start(bf16[10,4,4,128]{3,2,1,0:T(4,128)(2,1)S(1)} %get-tuple-element.17), channel_id=1, source_target_pairs={{8,0},{16,8},{24,16},{0,24},{9,1},{17,9},{25,17},{1,25},{10,2},{18... | collective-permute-start | bytes 122888 | tf_op jit(solution)/shard_map/ppermute | solution.py:24
  53.7 0.3 bitcast_multiply_fusion
  54.1 1.4 %collective-permute-done.8 = bf16[10,4,4,128]{3,2,1,0:T(4,128)(2,1)S(1)} collective-permute-done((bf16[10,4,4,128]{3,2,1,0:T(4,128)(2,1)S(1)}, bf16[10,4,4,128]{3,2,1,0:T(4,128)(2,1)S(1)}, u32[]{:S(2)}, u32[]{:S(2)}) %collective-permute-start.8) | collective-permute-done | bytes 40992 | tf_op jit(solution)/shard_map/ppermute | solution.py:21
  55.9 4.7 %collective-permute-start.11 = (bf16[10,4,24,4]{3,2,1,0:T(8,128)(2,1)S(1)}, bf16[10,4,24,4]{3,2,1,0:T(8,128)(2,1)S(1)}, u32[]{:S(2)}, u32[]{:S(2)}) collective-permute-start(bf16[10,4,24,4]{3,2,1,0:T(8,128)(2,1)S(1)} %get-tuple-element.19), channel_id=1, source_target_pairs={{1,0},{2,1},{3,2},{4,3},{5,4},{6,5},{7,6},{0,7},{9,8},{10,9},{11,1... | collective-permute-start | bytes 23048 | tf_op jit(solution)/shard_map/ppermute | solution.py:24
  60.6 6.0 %collective-permute-done.10 = bf16[10,4,24,4]{3,2,1,0:T(8,128)(2,1)S(1)} collective-permute-done((bf16[10,4,24,4]{3,2,1,0:T(8,128)(2,1)S(1)}, bf16[10,4,24,4]{3,2,1,0:T(8,128)(2,1)S(1)}, u32[]{:S(2)}, u32[]{:S(2)}) %collective-permute-start.10) | collective-permute-done | bytes 7712 | tf_op jit(solution)/shard_map/ppermute | solution.py:21
  66.7 2.5 %collective-permute-done.11 = bf16[10,4,24,4]{3,2,1,0:T(8,128)(2,1)S(1)} collective-permute-done((bf16[10,4,24,4]{3,2,1,0:T(8,128)(2,1)S(1)}, bf16[10,4,24,4]{3,2,1,0:T(8,128)(2,1)S(1)}, u32[]{:S(2)}, u32[]{:S(2)}) %collective-permute-start.11) | collective-permute-done | bytes 7712 | tf_op jit(solution)/shard_map/ppermute | solution.py:24
  69.2 0.5 maximum_select_fusion
  69.7 44.1 %add_convert_fusion = bf16[10,4,16,128]{3,2,1,0:T(8,128)(2,1)} fusion(f32[4,16,128]{2,1,0:T(8,128)S(1)} %get-tuple-element.2, f32[4,16,128]{2,1,0:T(8,128)S(1)} %get-tuple-element.49, f32[4,16,128]{2,1,0:T(8,128)S(1)} %get-tuple-element.52, f32[4,16,128]{2,1,0:T(8,128)S(1)} %get-tuple-element.37, f32[4,16,128]{2,1,0:T(8,128)S(1)} %get-tuple-element.4, ...), kind=kLoop, calls=%fused_computation.592 | loop fusion | flops 145244160 | bytes 14811136 | tf_op jit(solution)/shard_map/convert_element_type | solution.py:145
  (42 shorter events, 2.8 us)
Async XLA Ops:
  0.6 7.3 %copy-start = (f32[3,4,16,128]{3,2,1,0:T(8,128)S(1)}, f32[3,4,16,128]{3,2,1,0:T(8,128)}, u32[]{:S(2)}) copy-start(f32[3,4,16,128]{3,2,1,0:T(8,128)} %param.4) | copy-start | bytes 294916
  1.5 6.4 %collective-permute-start = (f32[3,4,2,128]{3,2,1,0:T(2,128)S(1)}, f32[3,4,2,128]{3,2,1,0:T(2,128)S(1)}, u32[]{:S(2)}, u32[]{:S(2)}) collective-permute-start(f32[3,4,2,128]{3,2,1,0:T(2,128)S(1)} %get-tuple-element.98), channel_id=1, source_target_pairs={{0,8},{8,16},{16,24},{24,0},{1,9},{9,17},{17,25},{25,1},{2,10},{10... | collective-permute-start | bytes 36872 | tf_op jit(solution)/shard_map/ppermute | solution.py:21
  2.1 5.9 %collective-permute-start.1 = (f32[3,4,2,128]{3,2,1,0:T(2,128)S(1)}, f32[3,4,2,128]{3,2,1,0:T(2,128)S(1)}, u32[]{:S(2)}, u32[]{:S(2)}) collective-permute-start(f32[3,4,2,128]{3,2,1,0:T(2,128)S(1)} %get-tuple-element.99), channel_id=1, source_target_pairs={{8,0},{16,8},{24,16},{0,24},{9,1},{17,9},{25,17},{1,25},{10,2},{18... | collective-permute-start | bytes 36872 | tf_op jit(solution)/shard_map/ppermute | solution.py:24
  4.1 20.1 %collective-permute-start.4 = (bf16[10,4,16,128]{3,2,1,0:T(8,128)(2,1)}, bf16[10,4,16,128]{3,2,1,0:T(8,128)(2,1)S(1)}, u32[]{:S(2)}, u32[]{:S(2)}) collective-permute-start(bf16[10,4,16,128]{3,2,1,0:T(8,128)(2,1)} %param.3), channel_id=1, source_target_pairs={{0,1},{1,2},{2,3},{3,4},{4,5},{5,6},{6,7},{7,0},{8,9},{9,10},{10,1... | collective-permute-start | bytes 491528 | tf_op jit(solution)/shard_map/ppermute | solution.py:12
  8.1 9.0 %collective-permute-start.2 = (f32[3,4,20,2]{3,2,1,0:T(8,128)S(1)}, f32[3,4,20,2]{3,2,1,0:T(8,128)S(1)}, u32[]{:S(2)}, u32[]{:S(2)}) collective-permute-start(f32[3,4,20,2]{3,2,1,0:T(8,128)S(1)} %get-tuple-element.20), channel_id=1, source_target_pairs={{0,1},{1,2},{2,3},{3,4},{4,5},{5,6},{6,7},{7,0},{8,9},{9,10},{10,1... | collective-permute-start | bytes 5768 | tf_op jit(solution)/shard_map/ppermute | solution.py:21
  9.7 10.4 %collective-permute-start.3 = (f32[3,4,20,2]{3,2,1,0:T(8,128)S(1)}, f32[3,4,20,2]{3,2,1,0:T(8,128)S(1)}, u32[]{:S(2)}, u32[]{:S(2)}) collective-permute-start(f32[3,4,20,2]{3,2,1,0:T(8,128)S(1)} %get-tuple-element.21), channel_id=1, source_target_pairs={{1,0},{2,1},{3,2},{4,3},{5,4},{6,5},{7,6},{0,7},{9,8},{10,9},{11,1... | collective-permute-start | bytes 5768 | tf_op jit(solution)/shard_map/ppermute | solution.py:24
  22.3 1.9 %copy-start.2 = (bf16[10,4,16,128]{3,2,1,0:T(8,128)(2,1)S(1)}, bf16[10,4,16,128]{3,2,1,0:T(8,128)(2,1)}, u32[]{:S(2)}) copy-start(bf16[10,4,16,128]{3,2,1,0:T(8,128)(2,1)} %param.3) | copy-start | bytes 491524
  24.3 8.0 %collective-permute-start.5 = (bf16[10,4,16,128]{3,2,1,0:T(8,128)(2,1)S(1)}, bf16[10,4,16,128]{3,2,1,0:T(8,128)(2,1)S(1)}, u32[]{:S(2)}, u32[]{:S(2)}) collective-permute-start(bf16[10,4,16,128]{3,2,1,0:T(8,128)(2,1)S(1)} %broadcast_select_fusion), channel_id=1, source_target_pairs={{0,2},{1,3},{2,4},{3,5},{4,6},{5,7},{6,0},{7,1},{8,10},{9,11},{10,... | collective-permute-start | bytes 491528 | tf_op jit(solution)/shard_map/ppermute | solution.py:12
  32.4 7.9 %collective-permute-start.6 = (bf16[10,4,16,128]{3,2,1,0:T(8,128)(2,1)S(1)}, bf16[10,4,16,128]{3,2,1,0:T(8,128)(2,1)S(1)}, u32[]{:S(2)}, u32[]{:S(2)}) collective-permute-start(bf16[10,4,16,128]{3,2,1,0:T(8,128)(2,1)S(1)} %broadcast_select_fusion.1), channel_id=1, source_target_pairs={{0,4},{1,5},{2,6},{3,7},{4,0},{5,1},{6,2},{7,3},{8,12},{9,13},{10,... | collective-permute-start | bytes 491528 | tf_op jit(solution)/shard_map/ppermute | solution.py:12
  34.3 26.3 %copy-start.1 = (f32[3,4,16,128]{3,2,1,0:T(8,128)}, f32[3,4,16,128]{3,2,1,0:T(8,128)S(1)}, u32[]{:S(2)}) copy-start(f32[3,4,16,128]{3,2,1,0:T(8,128)S(1)} %multiply_add_fusion.4) | copy-start | bytes 294916
  40.4 8.9 %collective-permute-start.7 = (bf16[10,4,16,128]{3,2,1,0:T(8,128)(2,1)S(1)}, bf16[10,4,16,128]{3,2,1,0:T(8,128)(2,1)S(1)}, u32[]{:S(2)}, u32[]{:S(2)}) collective-permute-start(bf16[10,4,16,128]{3,2,1,0:T(8,128)(2,1)S(1)} %broadcast_select_fusion.2), channel_id=1, source_target_pairs={{0,1},{1,2},{2,3},{3,4},{4,5},{5,6},{6,7},{7,0},{8,9},{9,10},{10,1... | collective-permute-start | bytes 491528 | tf_op jit(solution)/shard_map/ppermute | solution.py:12
  51.9 3.6 %collective-permute-start.8 = (bf16[10,4,4,128]{3,2,1,0:T(4,128)(2,1)S(1)}, bf16[10,4,4,128]{3,2,1,0:T(4,128)(2,1)S(1)}, u32[]{:S(2)}, u32[]{:S(2)}) collective-permute-start(bf16[10,4,4,128]{3,2,1,0:T(4,128)(2,1)S(1)} %get-tuple-element.16), channel_id=1, source_target_pairs={{0,8},{8,16},{16,24},{24,0},{1,9},{9,17},{17,25},{25,1},{2,10},{10... | collective-permute-start | bytes 122888 | tf_op jit(solution)/shard_map/ppermute | solution.py:21
  52.0 3.5 %collective-permute-start.9 = (bf16[10,4,4,128]{3,2,1,0:T(4,128)(2,1)S(1)}, bf16[10,4,4,128]{3,2,1,0:T(4,128)(2,1)S(1)}, u32[]{:S(2)}, u32[]{:S(2)}) collective-permute-start(bf16[10,4,4,128]{3,2,1,0:T(4,128)(2,1)S(1)} %get-tuple-element.17), channel_id=1, source_target_pairs={{8,0},{16,8},{24,16},{0,24},{9,1},{17,9},{25,17},{1,25},{10,2},{18... | collective-permute-start | bytes 122888 | tf_op jit(solution)/shard_map/ppermute | solution.py:24
  55.8 10.8 %collective-permute-start.10 = (bf16[10,4,24,4]{3,2,1,0:T(8,128)(2,1)S(1)}, bf16[10,4,24,4]{3,2,1,0:T(8,128)(2,1)S(1)}, u32[]{:S(2)}, u32[]{:S(2)}) collective-permute-start(bf16[10,4,24,4]{3,2,1,0:T(8,128)(2,1)S(1)} %get-tuple-element.18), channel_id=1, source_target_pairs={{0,1},{1,2},{2,3},{3,4},{4,5},{5,6},{6,7},{7,0},{8,9},{9,10},{10,1... | collective-permute-start | bytes 23048 | tf_op jit(solution)/shard_map/ppermute | solution.py:21
  55.9 13.3 %collective-permute-start.11 = (bf16[10,4,24,4]{3,2,1,0:T(8,128)(2,1)S(1)}, bf16[10,4,24,4]{3,2,1,0:T(8,128)(2,1)S(1)}, u32[]{:S(2)}, u32[]{:S(2)}) collective-permute-start(bf16[10,4,24,4]{3,2,1,0:T(8,128)(2,1)S(1)} %get-tuple-element.19), channel_id=1, source_target_pairs={{1,0},{2,1},{3,2},{4,3},{5,4},{6,5},{7,6},{0,7},{9,8},{10,9},{11,1... | collective-permute-start | bytes 23048 | tf_op jit(solution)/shard_map/ppermute | solution.py:24
where the time goes:
time: 114 us
  other arithmetic  54.9 us (48%)
  waiting for transfers between devices  39.5 us (35%)
  starting transfers between devices  16.3 us (14%)
  local copies, waits for them, and re-layouts  2.18 us (2%)
    convert_element_type x1, other arithmetic, local(): return (result.astype(jnp.bfloat16), disp)  44.1 us
    ppermute x4, waiting for transfers between devices, shifted_2(): lax.ppermute(x, axis, [(i, (i + by) % length) for i in range(length)])  22.3 us
    ppermute x4, starting transfers between devices, padded(): lax.ppermute(lax.slice_in_dim(block, 0, width, axis=dim), axis, backward)  11.6 us
    ppermute x4, waiting for transfers between devices, padded(): lax.ppermute(lax.slice_in_dim(block, block.shape[dim] - width, None, axis...  11.6 us
    ppermute x4, waiting for transfers between devices, padded(): lax.ppermute(lax.slice_in_dim(block, 0, width, axis=dim), axis, backward)  5.6 us
    add x3, other arithmetic, local(): total = total + wind_z_weights[wind_iz] * wind_plane  5.55 us
    ppermute x4, starting transfers between devices, shifted_2(): lax.ppermute(x, axis, [(i, (i + by) % length) for i in range(length)])  2.4 us
  transfers between devices with their start and end apart: 12, of which 8 were waited for; matrix products, arithmetic and copies ran while one was open for 7% of the time, Pallas kernels for 0%

commit v1 on v0

v1 whole, which is shorter than its diff:
```python
import functools

import jax
import jax.numpy as jnp
from jax import lax
from jax.experimental import pallas as pl
from jax.experimental.pallas import tpu as pltpu
from jax.sharding import PartitionSpec as P

ITERS = 3
RIM = 4
SUB = 8
MESH = pl.DeviceIdType.MESH


def cubic_weights(frac):
    return (
        -frac * (frac - 1.0) * (frac - 2.0) / 6.0,
        (frac + 1.0) * (frac - 1.0) * (frac - 2.0) / 2.0,
        -(frac + 1.0) * frac * (frac - 2.0) / 2.0,
        (frac + 1.0) * frac * (frac - 1.0) / 6.0,
    )


def spread(base, weights, lowest, highest):
    listed = []
    for target in range(lowest, highest + 1):
        summed = jnp.zeros(base.shape, jnp.float32)
        for a in range(len(weights)):
            summed = summed + jnp.where(base == float(target - a), weights[a], 0.0)
        listed.append(summed)
    return listed


def exchange_kernel(
    nlat, nlon, levels, t_ref, w_ref, s_ref, g_ref, s_out, d_ref,
    edge, edges, wind_n, wind_s, wide,
    sem_z, sem_x, sem_n, sem_s, got, got_n, got_s, own_sem,
    sem_w, got_w, sem_i, got_i,
):
    rows, _, cols = t_ref.shape
    planes = w_ref.shape[0]
    lat = lax.axis_index("lat")
    lon = lax.axis_index("lon")
    zc = nlon // 2
    zi = lon // 2
    xi = lon % 2
    north = (lat + nlat - 1) % nlat
    south = (lat + 1) % nlat
    east = (lon + 1) % nlon
    west = (lon + nlon - 1) % nlon
    partner = zi * 2 + (1 - xi)

    def peer(j):
        return ((zi + j) % zc) * 2 + xi

    around = [(lat, east), (lat, west), (north, east), (north, west), (south, east), (south, west)]
    targets = [(north, lon), (south, lon), (lat, partner)] + around
    targets += [(lat, peer(j)) for j in range(1, zc)]
    barrier = pltpu.get_barrier_semaphore()
    for target in targets:
        pl.semaphore_signal(barrier, inc=1, device_id=target, device_id_type=MESH)

    lane = lax.broadcasted_iota(jnp.int32, (rows, cols), 1)
    packed = jnp.zeros((rows, cols), jnp.float32)
    for c in range(planes):
        turned = pltpu.roll(w_ref[c], (2 + 4 * c) % cols, 1)
        packed = jnp.where((lane >= 4 * c) & (lane < 4 * c + 4), turned, packed)
    edge[...] = packed
    s_out[RIM : RIM + rows] = s_ref[...]
    pl.semaphore_wait(barrier, len(targets))

    def remote(src, dst, send, recv, target):
        copy = pltpu.make_async_remote_copy(
            src_ref=src, dst_ref=dst, send_sem=send, recv_sem=recv,
            device_id=target, device_id_type=MESH,
        )
        copy.start()
        return copy

    sends = []
    winds = []
    for n, target in enumerate(around):
        slot = (1, 0, 5, 4, 3, 2)[n]
        winds.append(remote(edge, edges.at[slot], sem_w.at[n], got_w.at[slot], target))
    winds.append(remote(w_ref.at[:, 0:SUB], wind_s, sem_w.at[6], got_w.at[6], (north, lon)))
    winds.append(remote(w_ref.at[:, rows - SUB : rows], wind_n, sem_w.at[7], got_w.at[7], (south, lon)))
    winds.append(remote(s_ref.at[0:RIM], s_out.at[RIM + rows : RIM + rows + RIM], sem_i.at[0], got_i.at[0], (north, lon)))
    winds.append(remote(s_ref.at[rows - RIM : rows], s_out.at[0:RIM], sem_i.at[1], got_i.at[1], (south, lon)))

    body = pl.ds(RIM, rows)
    sends.append(remote(t_ref, g_ref.at[lon, body], sem_x.at[lon], got.at[lon], (lat, partner)))
    for j in [j for pair in zip(range(1, zc), range(zc - 1, 0, -1)) for j in pair][: zc - 1]:
        sends.append(remote(t_ref, g_ref.at[lon, body], sem_z.at[j], got.at[lon], (lat, peer(j))))

    def rims(p, src, first):
        sends.append(remote(src.at[first : first + RIM], g_ref.at[p, RIM + rows : RIM + rows + RIM], sem_n.at[p], got_n.at[p], (north, lon)))
        sends.append(remote(src.at[first + rows - RIM : first + rows], g_ref.at[p, 0:RIM], sem_s.at[p], got_s.at[p], (south, lon)))

    rims(lon, t_ref, 0)
    own = pltpu.make_async_copy(t_ref, g_ref.at[lon, body], own_sem)
    own.start()

    def arrived(p):
        pltpu.make_async_remote_copy(
            src_ref=g_ref.at[p, body], dst_ref=g_ref.at[p, body], send_sem=own_sem, recv_sem=got.at[p],
            device_id=(lat, partner), device_id_type=MESH,
        ).wait_recv()

    def relay(j):
        p = ((zi + zc - j) % zc) * 2 + xi
        arrived(p)
        sends.append(remote(g_ref.at[p, body], g_ref.at[p, body], sem_x.at[p], got.at[p], (lat, partner)))
        rims(p, g_ref.at[p], RIM)

    def pass_rims(j):
        p = ((zi + zc - j) % zc) * 2 + (1 - xi)
        arrived(p)
        rims(p, g_ref.at[p], RIM)

    for copy in winds:
        copy.wait()

    tall = rows + 2 * SUB
    total_rows = rows * nlat
    tall_lane = lax.broadcasted_iota(jnp.int32, (tall, cols), 1)
    rowpos = lax.broadcasted_iota(jnp.int32, (tall, cols), 0) + (lat * rows - SUB)
    inside = (rowpos >= 0) & (rowpos < total_rows)
    from_east = jnp.concatenate([edges[2][rows - SUB :], edges[0], edges[4][:SUB]], axis=0)
    from_west = jnp.concatenate([edges[3][rows - SUB :], edges[1], edges[5][:SUB]], axis=0)
    for c in range(planes):
        block = jnp.concatenate([wind_n[c], w_ref[c], wind_s[c]], axis=0)
        for d in range(-2, 3):
            if d > 0:
                value = jnp.where(
                    tall_lane >= cols - d,
                    pltpu.roll(from_east, (cols - 2 - d - 4 * c) % cols, 1),
                    pltpu.roll(block, cols - d, 1),
                )
            elif d < 0:
                value = jnp.where(
                    tall_lane < -d,
                    pltpu.roll(from_west, (-d - 2 - 4 * c) % cols, 1),
                    pltpu.roll(block, -d, 1),
                )
            else:
                value = block
            wide[d + 2, c] = jnp.where(inside, value, 0.0)

    def trajectory(k):
        for b in range(rows // SUB):
            near = slice(b * SUB, (b + 1) * SUB)
            growi = lax.broadcasted_iota(jnp.int32, (SUB, cols), 0) + (lat * rows + b * SUB)
            gpos = growi.astype(jnp.float32)

            def step(_, disp):
                zlev = jnp.clip(float(k) - 0.5 * disp[0], 0.0, levels - 1.0)
                ylat = jnp.clip(gpos - 0.5 * disp[1], 0.0, total_rows - 1.0)
                xrel = -0.5 * disp[2]
                zb = jnp.floor(zlev)
                yb = jnp.floor(ylat)
                xb = jnp.floor(xrel)
                tz = zlev - zb
                ty = ylat - yb
                tx = xrel - xb
                wz = spread(zb, (1.0 - tz, tz), 0, levels - 1)
                wy = spread(yb - gpos, (1.0 - ty, ty), -2, 2)
                wx = spread(xb, (1.0 - tx, tx), -2, 2)
                result = []
                for comp in range(3):
                    total = None
                    for z in range(levels):
                        plane = None
                        for y in range(5):
                            start = SUB + b * SUB + y - 2
                            line = None
                            for x in range(5):
                                term = wx[x] * wide[x, comp * levels + z, start : start + SUB]
                                line = term if line is None else line + term
                            term = wy[y] * line
                            plane = term if plane is None else plane + term
                        term = wz[z] * plane
                        total = term if total is None else total + term
                    result.append(total)
                return tuple(result)

            disp = tuple(w_ref[comp * levels + k, near] for comp in range(3))
            disp = lax.fori_loop(0, ITERS, step, disp)
            for comp in range(3):
                d_ref[comp * levels + k, near] = disp[comp]

    order = [j for pair in zip(range(1, zc), range(zc - 1, 0, -1)) for j in pair][: zc - 1]
    for n in range(max(levels, len(order))):
        if n < len(order):
            relay(order[n])
        if n < levels:
            trajectory(n)
    pass_rims(0)
    for j in order:
        pass_rims(j)
    own.wait()
    for copy in sends:
        copy.wait_send()
    for p in range(nlon):
        for dst, sem in ((g_ref.at[p, RIM + rows : RIM + rows + RIM], got_n), (g_ref.at[p, 0:RIM], got_s)):
            pltpu.make_async_remote_copy(
                src_ref=dst, dst_ref=dst, send_sem=own_sem, recv_sem=sem.at[p],
                device_id=(north, lon), device_id_type=MESH,
            ).wait_recv()


def stencil_kernel(nlat, nlon, levels, rows, s_ref, d_ref, g_ref, o_ref, window, shifted, result, sems):
    high, fields, cols = g_ref.shape[1:]
    ntrac = fields // levels
    lat = lax.axis_index("lat")
    lon = lax.axis_index("lon")
    total_rows = rows * nlat

    def place(r):
        first = lon * cols - RIM - s_ref[r, 0, 0] + 2 * nlon * cols
        return first // cols, first % cols

    def fetch(r, n):
        sector = (place(r)[0] + n) % nlon
        return pltpu.make_async_copy(g_ref.at[sector, r], window.at[r, n], sems.at[r])

    def start(r, _):
        for n in range(3):
            fetch(r, n).start()
        return 0

    lax.fori_loop(0, high, start, 0)
    lane = lax.broadcasted_iota(jnp.int32, (fields, cols), 1)

    def turn(r, _):
        pltpu.make_async_copy(g_ref.at[0:3, r], window.at[r], sems.at[r]).wait()
        offset = place(r)[1]
        rowpos = lat * rows - RIM + r
        inside = (rowpos >= 0) & (rowpos < total_rows)
        amount = (cols - offset) % cols
        turned = [pltpu.roll(window[r, n].astype(jnp.float32), amount, 1) for n in range(3)]
        early = lane < cols - offset
        keep = jnp.full((fields, cols), inside)
        low = jnp.where(keep, jnp.where(early, turned[0], turned[1]), 0.0)
        high_part = jnp.where(keep, jnp.where(early, turned[1], turned[2]), 0.0)
        for d in range(2 * RIM + 1):
            value = low
            if d > 0:
                value = jnp.where(
                    lane < cols - d, pltpu.roll(low, cols - d, 1), pltpu.roll(high_part, cols - d, 1)
                )
            shifted[d, pl.ds(r, fields, stride=high), :] = value
        return 0

    lax.fori_loop(0, high, turn, 0)
    wide = 2 * RIM + 1
    for k in range(levels):
        for b in range(rows // SUB):
            near = slice(b * SUB, (b + 1) * SUB)
            growi = lax.broadcasted_iota(jnp.int32, (SUB, cols), 0) + (lat * rows + b * SUB)
            gpos = growi.astype(jnp.float32)
            zdep = jnp.clip(float(k) - d_ref[k, near], 0.0, levels - 1.0)
            ydep = jnp.clip(gpos - d_ref[levels + k, near], 0.0, total_rows - 1.0)
            xrel = -d_ref[2 * levels + k, near]
            zb = jnp.floor(zdep)
            yb = jnp.floor(ydep)
            xb = jnp.floor(xrel)
            wz = spread(zb - 1.0, cubic_weights(zdep - zb), 0, levels - 1)
            wy = spread(yb - gpos - 1.0, cubic_weights(ydep - yb), -RIM, RIM)
            wx = spread(xb - 1.0, cubic_weights(xrel - xb), -RIM, RIM)

            def tracer(t, _):
                total = None
                for z in range(levels):
                    base = pl.multiple_of((t * levels + z) * high + b * SUB, SUB)
                    plane = None
                    for y in range(wide):
                        line = None
                        for x in range(wide):
                            term = wx[x] * shifted[x, pl.ds(base + y, SUB), :]
                            line = term if line is None else line + term
                        term = wy[y] * line
                        plane = term if plane is None else plane + term
                    term = wz[z] * plane
                    total = term if total is None else total + term
                result[t * levels + k, near] = total
                return 0

            lax.fori_loop(0, ntrac, tracer, 0)
    o_ref[...] = result[...].astype(o_ref.dtype)


def local(tracers, winds, zonal_shift):
    ntrac, levels, rows, cols = tracers.shape
    nlat = lax.axis_size("lat")
    nlon = lax.axis_size("lon")
    fields = ntrac * levels
    planes = 3 * levels
    high = rows + 2 * RIM
    dma = pltpu.SemaphoreType.DMA
    vmem = pl.BlockSpec(memory_space=pltpu.VMEM)
    any_space = pl.BlockSpec(memory_space=pl.ANY)
    by_row = jnp.transpose(tracers.reshape(fields, rows, cols), (1, 0, 2))
    shift_rows = jnp.broadcast_to(zonal_shift[:, None, None], (rows, 1, 128))
    gathered, shifts, disp = pl.pallas_call(
        functools.partial(exchange_kernel, nlat, nlon, levels),
        out_shape=(
            jax.ShapeDtypeStruct((nlon, high, fields, cols), tracers.dtype),
            jax.ShapeDtypeStruct((high, 1, 128), jnp.int32),
            jax.ShapeDtypeStruct((planes, rows, cols), jnp.float32),
        ),
        in_specs=[vmem, vmem, vmem],
        out_specs=(any_space, vmem, vmem),
        scratch_shapes=[
            pltpu.VMEM((rows, cols), jnp.float32),
            pltpu.VMEM((6, rows, cols), jnp.float32),
            pltpu.VMEM((planes, SUB, cols), jnp.float32),
            pltpu.VMEM((planes, SUB, cols), jnp.float32),
            pltpu.VMEM((5, planes, rows + 2 * SUB, cols), jnp.float32),
            dma((nlon,)), dma((nlon,)), dma((nlon,)), dma((nlon,)),
            dma((nlon,)), dma((nlon,)), dma((nlon,)), dma,
            dma((8,)), dma((8,)), dma((2,)), dma((2,)),
        ],
        compiler_params=pltpu.CompilerParams(collective_id=0, has_side_effects=True),
        name="exchange",
    )(by_row, winds.reshape(planes, rows, cols), shift_rows)
    out = pl.pallas_call(
        functools.partial(stencil_kernel, nlat, nlon, levels, rows),
        out_shape=jax.ShapeDtypeStruct((fields, rows, cols), tracers.dtype),
        in_specs=[pl.BlockSpec(memory_space=pltpu.SMEM), vmem, any_space],
        out_specs=vmem,
        scratch_shapes=[
            pltpu.VMEM((high, 3, fields, cols), tracers.dtype),
            pltpu.VMEM((2 * RIM + 1, fields * high, cols), jnp.float32),
            pltpu.VMEM((fields, rows, cols), jnp.float32),
            dma((high,)),
        ],
        name="stencil",
    )(shifts, disp, gathered)
    return out.reshape(tracers.shape), disp.reshape(winds.shape)


def solution(mesh):
    return jax.shard_map(
        local,
        mesh=mesh,
        in_specs=(P(None, None, "lat", "lon"), P(None, None, "lat", "lon"), P("lat")),
        out_specs=(P(None, None, "lat", "lon"), P(None, None, "lat", "lon")),
        check_vma=False,
    )
```

time: 114 us -> 57.3 us (0.50)
  other arithmetic: 54.9 us -> 0 us
  Pallas kernels: 0 us -> 52.7 us
  waiting for transfers between devices: 39.5 us -> 0 us
  starting transfers between devices: 16.3 us -> 0 us
  local copies, waits for them, and re-layouts: 2.18 us -> 3.63 us
    pallas_call x0 -> x2, Pallas kernels: none -> 52.7 us  [the longest x1 32.8 us: local(): pl.pallas_call(functools.partial(exchange_kernel, nlat, nlon, levels), ou...]
    convert_element_type x1 -> x0, other arithmetic: 44.1 us -> none  [local(): return (result.astype(jnp.bfloat16), disp)]
    ppermute x12 -> x0, waiting for transfers between devices: 39.5 us -> none  [the longest x4 22.3 us: shifted_2(): lax.ppermute(x, axis, [(i, (i + by) % length) for i in range(length)])]
    ppermute x12 -> x0, starting transfers between devices: 16.3 us -> none  [the longest x4 11.6 us: padded(): lax.ppermute(lax.slice_in_dim(block, 0, width, axis=dim), axis, backward)]
    add x4 -> x0, other arithmetic: 5.55 us -> none  [the longest x3 5.55 us: local(): total = total + wind_z_weights[wind_iz] * wind_plane]
    select_n x13 -> x0, other arithmetic: 2.31 us -> none  [the longest x8 1.29 us: translate_doubling(): joined = jnp.where(chosen, shifted, joined)]
    unnamed x6 -> x4, local copies, waits for them, and re-layouts: 0.02 us -> 2.29 us
    slice x12 -> x0, local copies, waits for them, and re-layouts: 2.16 us -> none  [the longest x4 1.14 us: padded(): lax.slice_in_dim(block, block.shape[dim] - width, None, axis=dim)]
  transfers between devices with their start and end apart: 12 -> 0, of which waited for: 8 -> 0; matrix products, arithmetic and copies ran while one was open for 7% -> 0% of each run, Pallas kernels for 0% -> 0%
where the time goes in v1:
time: 57.3 us; the launch traced here: 57 us
  Pallas kernels  52.7 us (92%)
  local copies, waits for them, and re-layouts  3.63 us (6%)
  between operations  0.66 us (1%)
    pallas_call x1, Pallas kernels, local(): pl.pallas_call(functools.partial(exchange_kernel, nlat, nlon, levels), ou...  32.8 us
    pallas_call x1, Pallas kernels, local(): pl.pallas_call(functools.partial(stencil_kernel, nlat, nlon, levels, rows...  19.9 us
    unnamed x4, local copies, waits for them, and re-layouts  2.29 us
    broadcast_in_dim x1, local copies, waits for them, and re-layouts, local(): shift_rows = jnp.broadcast_to(zonal_shift[:, None, None], (rows, 1, 128))  1.34 us

profile of v1, /device:TPU:0, one launch (start us, length us, event | category | flops | bytes accessed | tf_op | source)
XLA Modules:
  0.0 57.0 jit_solution(4434842136237385837)
XLA Ops:
  0.6 1.3 %broadcast_in_dim.2.s_ref = s32[16,1,128]{2,1,0:T(1,128)} broadcast(s32[16]{0:T(128)} %param.5), dimensions={0} | broadcast | bytes 8256 | tf_op jit(solution)/shard_map/broadcast_in_dim | solution.py:304
  2.0 1.6 %copy.5 = bf16[10,4,16,128]{3,1,0,2:T(4,128)(2,1)} copy(bf16[10,4,16,128]{3,2,1,0:T(8,128)(2,1)} %param.3) | data formatting | bytes 327680 | tf_op args[0]
  3.6 32.8 %exchange.1 = (bf16[8,24,40,128]{3,2,1,0:T(8,128)(2,1)}, s32[24,1,128]{2,1,0:T(1,128)}, f32[12,16,128]{2,1,0:T(8,128)}) custom-call(bf16[16,40,128]{2,1,0:T(8,128)(2,1)} %bitcast.6, f32[12,16,128]{2,1,0:T(8,128)} %bitcast.9, s32[16,1,128]{2,1,0:T(1,128)} %broadcast_in_dim.2.s_ref), custom_call_target="tpu_custom_call" | custom-call | tf_op jit(solution)/shard_map/exchange/pallas_call | solution.py:305
  36.4 0.0 copy-start
  36.4 19.9 %stencil.1 = bf16[40,16,128]{2,1,0:T(8,128)(2,1)} custom-call(s32[24,1,128]{2,1,0:T(1,128)} %get-tuple-element.5.s_ref, f32[12,16,128]{2,1,0:T(8,128)} %get-tuple-element.6.d_ref, bf16[8,24,40,128]{3,2,1,0:T(8,128)(2,1)} %get-tuple-element.7.g_ref), custom_call_target="tpu_custom_call" | custom-call | tf_op jit(solution)/shard_map/stencil/pallas_call | solution.py:327
  56.3 0.0 copy-done
  56.4 0.6 %copy.7 = f32[3,4,16,128]{3,2,1,0:T(8,128)} copy(f32[3,4,16,128]{3,2,1,0:T(8,128)S(1)} %bitcast.7) | data formatting | bytes 196608
Async XLA Ops:
  36.4 19.9 %copy-start = (f32[12,16,128]{2,1,0:T(8,128)S(1)}, f32[12,16,128]{2,1,0:T(8,128)}, u32[]{:S(2)}) copy-start(f32[12,16,128]{2,1,0:T(8,128)} %get-tuple-element.6.d_ref) | copy-start | bytes 294916

commit v2 on v1

--- a/solution.py
+++ b/solution.py
@@ -67,7 +67,8 @@
         turned = pltpu.roll(w_ref[c], (2 + 4 * c) % cols, 1)
         packed = jnp.where((lane >= 4 * c) & (lane < 4 * c + 4), turned, packed)
     edge[...] = packed
-    s_out[RIM : RIM + rows] = s_ref[...]
+    for r in range(rows):
+        s_out[RIM + r] = jnp.full(s_out.shape[1:], s_ref[r])
     pl.semaphore_wait(barrier, len(targets))
 
     def remote(src, dst, send, recv, target):
@@ -85,38 +86,51 @@
         winds.append(remote(edge, edges.at[slot], sem_w.at[n], got_w.at[slot], target))
     winds.append(remote(w_ref.at[:, 0:SUB], wind_s, sem_w.at[6], got_w.at[6], (north, lon)))
     winds.append(remote(w_ref.at[:, rows - SUB : rows], wind_n, sem_w.at[7], got_w.at[7], (south, lon)))
-    winds.append(remote(s_ref.at[0:RIM], s_out.at[RIM + rows : RIM + rows + RIM], sem_i.at[0], got_i.at[0], (north, lon)))
-    winds.append(remote(s_ref.at[rows - RIM : rows], s_out.at[0:RIM], sem_i.at[1], got_i.at[1], (south, lon)))
-
-    body = pl.ds(RIM, rows)
-    sends.append(remote(t_ref, g_ref.at[lon, body], sem_x.at[lon], got.at[lon], (lat, partner)))
-    for j in [j for pair in zip(range(1, zc), range(zc - 1, 0, -1)) for j in pair][: zc - 1]:
-        sends.append(remote(t_ref, g_ref.at[lon, body], sem_z.at[j], got.at[lon], (lat, peer(j))))
-
-    def rims(p, src, first):
-        sends.append(remote(src.at[first : first + RIM], g_ref.at[p, RIM + rows : RIM + rows + RIM], sem_n.at[p], got_n.at[p], (north, lon)))
-        sends.append(remote(src.at[first + rows - RIM : first + rows], g_ref.at[p, 0:RIM], sem_s.at[p], got_s.at[p], (south, lon)))
-
-    rims(lon, t_ref, 0)
-    own = pltpu.make_async_copy(t_ref, g_ref.at[lon, body], own_sem)
+    own_rows = s_out.at[RIM : RIM + rows]
+    winds.append(remote(own_rows.at[0:RIM], s_out.at[RIM + rows : RIM + rows + RIM], sem_i.at[0], got_i.at[0], (north, lon)))
+    winds.append(remote(own_rows.at[rows - RIM : rows], s_out.at[0:RIM], sem_i.at[1], got_i.at[1], (south, lon)))
+
+    pieces = rows // RIM
+    piece_order = [0, pieces - 1] + list(range(1, pieces - 1))
+    order = [j for pair in zip(range(1, zc), range(zc - 1, 0, -1)) for j in pair][: zc - 1]
+
+    def part(c):
+        return pl.ds(RIM + c * RIM, RIM)
+
+    def rims(p, c, src):
+        if c == 0:
+            sends.append(remote(src, g_ref.at[p, RIM + rows : RIM + rows + RIM], sem_n.at[p], got_n.at[p], (north, lon)))
+        if c == pieces - 1:
+            sends.append(remote(src, g_ref.at[p, 0:RIM], sem_s.at[p], got_s.at[p], (south, lon)))
+
+    for c in piece_order:
+        mine = t_ref.at[c * RIM : (c + 1) * RIM]
+        sends.append(remote(mine, g_ref.at[lon, part(c)], sem_x.at[lon, c], got.at[lon, c], (lat, partner)))
+        for j in order:
+            sends.append(remote(mine, g_ref.at[lon, part(c)], sem_z.at[j, c], got.at[lon, c], (lat, peer(j))))
+        rims(lon, c, mine)
+    own = pltpu.make_async_copy(t_ref, g_ref.at[lon, RIM : RIM + rows], own_sem)
     own.start()
 
-    def arrived(p):
+    def arrived(p, c):
         pltpu.make_async_remote_copy(
-            src_ref=g_ref.at[p, body], dst_ref=g_ref.at[p, body], send_sem=own_sem, recv_sem=got.at[p],
+            src_ref=g_ref.at[p, part(c)], dst_ref=g_ref.at[p, part(c)], send_sem=own_sem, recv_sem=got.at[p, c],
             device_id=(lat, partner), device_id_type=MESH,
         ).wait_recv()
 
-    def relay(j):
-        p = ((zi + zc - j) % zc) * 2 + xi
-        arrived(p)
-        sends.append(remote(g_ref.at[p, body], g_ref.at[p, body], sem_x.at[p], got.at[p], (lat, partner)))
-        rims(p, g_ref.at[p], RIM)
-
-    def pass_rims(j):
-        p = ((zi + zc - j) % zc) * 2 + (1 - xi)
-        arrived(p)
-        rims(p, g_ref.at[p], RIM)
+    def relay(c):
+        for j in order:
+            p = ((zi + zc - j) % zc) * 2 + xi
+            arrived(p, c)
+            piece = g_ref.at[p, part(c)]
+            sends.append(remote(piece, piece, sem_x.at[p, c], got.at[p, c], (lat, partner)))
+            rims(p, c, piece)
+
+    def pass_rims(c):
+        for j in [0] + order:
+            p = ((zi + zc - j) % zc) * 2 + (1 - xi)
+            arrived(p, c)
+            rims(p, c, g_ref.at[p, part(c)])
 
     for copy in winds:
         copy.wait()
@@ -189,15 +203,14 @@
             for comp in range(3):
                 d_ref[comp * levels + k, near] = disp[comp]
 
-    order = [j for pair in zip(range(1, zc), range(zc - 1, 0, -1)) for j in pair][: zc - 1]
-    for n in range(max(levels, len(order))):
-        if n < len(order):
-            relay(order[n])
+    for n in range(max(levels, pieces)):
         if n < levels:
             trajectory(n)
-    pass_rims(0)
-    for j in order:
-        pass_rims(j)
+        if n < pieces:
+            relay(piece_order[n])
+            if n > 0:
+                pass_rims(piece_order[n - 1])
+    pass_rims(piece_order[-1])
     own.wait()
     for copy in sends:
         copy.wait_send()
@@ -301,7 +314,7 @@
     vmem = pl.BlockSpec(memory_space=pltpu.VMEM)
     any_space = pl.BlockSpec(memory_space=pl.ANY)
     by_row = jnp.transpose(tracers.reshape(fields, rows, cols), (1, 0, 2))
-    shift_rows = jnp.broadcast_to(zonal_shift[:, None, None], (rows, 1, 128))
+    pieces = rows // RIM
     gathered, shifts, disp = pl.pallas_call(
         functools.partial(exchange_kernel, nlat, nlon, levels),
         out_shape=(
@@ -309,7 +322,7 @@
             jax.ShapeDtypeStruct((high, 1, 128), jnp.int32),
             jax.ShapeDtypeStruct((planes, rows, cols), jnp.float32),
         ),
-        in_specs=[vmem, vmem, vmem],
+        in_specs=[vmem, vmem, pl.BlockSpec(memory_space=pltpu.SMEM)],
         out_specs=(any_space, vmem, vmem),
         scratch_shapes=[
             pltpu.VMEM((rows, cols), jnp.float32),
@@ -317,13 +330,13 @@
             pltpu.VMEM((planes, SUB, cols), jnp.float32),
             pltpu.VMEM((planes, SUB, cols), jnp.float32),
             pltpu.VMEM((5, planes, rows + 2 * SUB, cols), jnp.float32),
-            dma((nlon,)), dma((nlon,)), dma((nlon,)), dma((nlon,)),
-            dma((nlon,)), dma((nlon,)), dma((nlon,)), dma,
+            dma((nlon, pieces)), dma((nlon, pieces)), dma((nlon,)), dma((nlon,)),
+            dma((nlon, pieces)), dma((nlon,)), dma((nlon,)), dma,
             dma((8,)), dma((8,)), dma((2,)), dma((2,)),
         ],
         compiler_params=pltpu.CompilerParams(collective_id=0, has_side_effects=True),
         name="exchange",
-    )(by_row, winds.reshape(planes, rows, cols), shift_rows)
+    )(by_row, winds.reshape(planes, rows, cols), zonal_shift)
     out = pl.pallas_call(
         functools.partial(stencil_kernel, nlat, nlon, levels, rows),
         out_shape=jax.ShapeDtypeStruct((fields, rows, cols), tracers.dtype),

time: 57.3 us -> 53.1 us (0.927)
  Pallas kernels: 52.7 us -> 50 us
  local copies, waits for them, and re-layouts: 3.63 us -> 2.29 us
    pallas_call x1, Pallas kernels: 32.8 us -> 30 us  [local(): pl.pallas_call(functools.partial(exchange_kernel, nlat, nlon, levels), ou...]
    broadcast_in_dim x1 -> x0, local copies, waits for them, and re-layouts: 1.34 us -> none  [local(): shift_rows = jnp.broadcast_to(zonal_shift[:, None, None], (rows, 1, 128))]
where the time goes in v2:
time: 53.1 us; the launch traced here: 52.9 us
  Pallas kernels  50 us (94%)
  local copies, waits for them, and re-layouts  2.29 us (4%)
  between operations  0.66 us (1%)
    pallas_call x1, Pallas kernels, local(): pl.pallas_call(functools.partial(exchange_kernel, nlat, nlon, levels), ou...  30 us
    pallas_call x1, Pallas kernels, local(): pl.pallas_call(functools.partial(stencil_kernel, nlat, nlon, levels, rows...  19.9 us
    unnamed x4, local copies, waits for them, and re-layouts  2.29 us

profile of v2, /device:TPU:0, one launch (start us, length us, event | category | flops | bytes accessed | tf_op | source)
XLA Modules:
  0.0 52.9 jit_solution(1410013715946765720)
XLA Ops:
  0.6 1.6 %copy.5 = bf16[10,4,16,128]{3,1,0,2:T(4,128)(2,1)} copy(bf16[10,4,16,128]{3,2,1,0:T(8,128)(2,1)} %param.3) | data formatting | bytes 327680 | tf_op args[0]
  2.3 30.0 %exchange.1 = (bf16[8,24,40,128]{3,2,1,0:T(8,128)(2,1)}, s32[24,1,128]{2,1,0:T(1,128)}, f32[12,16,128]{2,1,0:T(8,128)}) custom-call(bf16[16,40,128]{2,1,0:T(8,128)(2,1)} %bitcast.6, f32[12,16,128]{2,1,0:T(8,128)} %bitcast.9, s32[16]{0:T(128)} %s_ref.1), custom_call_target="tpu_custom_call" | custom-call | tf_op jit(solution)/shard_map/exchange/pallas_call | solution.py:318
  32.3 0.0 copy-start
  32.3 19.9 %stencil.1 = bf16[40,16,128]{2,1,0:T(8,128)(2,1)} custom-call(s32[24,1,128]{2,1,0:T(1,128)} %get-tuple-element.5.s_ref, f32[12,16,128]{2,1,0:T(8,128)} %get-tuple-element.6.d_ref, bf16[8,24,40,128]{3,2,1,0:T(8,128)(2,1)} %get-tuple-element.7.g_ref), custom_call_target="tpu_custom_call" | custom-call | tf_op jit(solution)/shard_map/stencil/pallas_call | solution.py:340
  52.3 0.0 copy-done
  52.3 0.6 %copy.7 = f32[3,4,16,128]{3,2,1,0:T(8,128)} copy(f32[3,4,16,128]{3,2,1,0:T(8,128)S(1)} %bitcast.7) | data formatting | bytes 196608
Async XLA Ops:
  32.3 19.9 %copy-start = (f32[12,16,128]{2,1,0:T(8,128)S(1)}, f32[12,16,128]{2,1,0:T(8,128)}, u32[]{:S(2)}) copy-start(f32[12,16,128]{2,1,0:T(8,128)} %get-tuple-element.6.d_ref) | copy-start | bytes 294916

commit v3 on v2

--- a/solution.py
+++ b/solution.py
@@ -222,9 +222,12 @@
             ).wait_recv()
 
 
-def stencil_kernel(nlat, nlon, levels, rows, s_ref, d_ref, g_ref, o_ref, window, shifted, result, sems):
+def stencil_kernel(nlat, nlon, levels, rows, s_ref, d_ref, g_ref, o_ref, window, source, band, wxs, wys, wzs, partial_sum, result, sems):
     high, fields, cols = g_ref.shape[1:]
     ntrac = fields // levels
+    pitch = source.shape[0] // high
+    wide = 2 * RIM + 1
+    turn_rows = band.shape[1]
     lat = lax.axis_index("lat")
     lon = lax.axis_index("lon")
     total_rows = rows * nlat
@@ -233,74 +236,87 @@
         first = lon * cols - RIM - s_ref[r, 0, 0] + 2 * nlon * cols
         return first // cols, first % cols
 
-    def fetch(r, n):
-        sector = (place(r)[0] + n) % nlon
-        return pltpu.make_async_copy(g_ref.at[sector, r], window.at[r, n], sems.at[r])
-
     def start(r, _):
+        base = place(r)[0]
         for n in range(3):
-            fetch(r, n).start()
+            pltpu.make_async_copy(g_ref.at[(base + n) % nlon, r], window.at[r, n], sems.at[r]).start()
         return 0
 
     lax.fori_loop(0, high, start, 0)
+
+    gpos = (lax.broadcasted_iota(jnp.int32, (rows, cols), 0) + lat * rows).astype(jnp.float32)
+    for k in range(levels):
+        zdep = jnp.clip(float(k) - d_ref[k], 0.0, levels - 1.0)
+        ydep = jnp.clip(gpos - d_ref[levels + k], 0.0, total_rows - 1.0)
+        xrel = -d_ref[2 * levels + k]
+        zb = jnp.floor(zdep)
+        yb = jnp.floor(ydep)
+        xb = jnp.floor(xrel)
+        for z, value in enumerate(spread(zb - 1.0, cubic_weights(zdep - zb), 0, levels - 1)):
+            wzs[k * levels + z] = value
+        for y, value in enumerate(spread(yb - gpos - 1.0, cubic_weights(ydep - yb), -RIM, RIM)):
+            wys[k * wide + y] = value
+        for x, value in enumerate(spread(xb - 1.0, cubic_weights(xrel - xb), -RIM, RIM)):
+            wxs[k, x * rows : (x + 1) * rows] = value
+        for x in range(wide, turn_rows):
+            wxs[k, x * rows : (x + 1) * rows] = jnp.zeros((rows, cols), jnp.float32)
+    blocks = band.shape[0]
+    row_at = lax.broadcasted_iota(jnp.int32, (turn_rows, cols), 0)
+    col_at = lax.broadcasted_iota(jnp.int32, (turn_rows, cols), 1)
+    for m in range(blocks):
+        apart = row_at + m * turn_rows - col_at
+        band[m] = jnp.where((apart >= 0) & (apart < turn_rows), 1.0, 0.0).astype(band.dtype)
+
     lane = lax.broadcasted_iota(jnp.int32, (fields, cols), 1)
 
     def turn(r, _):
         pltpu.make_async_copy(g_ref.at[0:3, r], window.at[r], sems.at[r]).wait()
         offset = place(r)[1]
         rowpos = lat * rows - RIM + r
-        inside = (rowpos >= 0) & (rowpos < total_rows)
+        keep = jnp.full((fields, cols), (rowpos >= 0) & (rowpos < total_rows))
         amount = (cols - offset) % cols
         turned = [pltpu.roll(window[r, n].astype(jnp.float32), amount, 1) for n in range(3)]
         early = lane < cols - offset
-        keep = jnp.full((fields, cols), inside)
-        low = jnp.where(keep, jnp.where(early, turned[0], turned[1]), 0.0)
-        high_part = jnp.where(keep, jnp.where(early, turned[1], turned[2]), 0.0)
-        for d in range(2 * RIM + 1):
-            value = low
-            if d > 0:
-                value = jnp.where(
-                    lane < cols - d, pltpu.roll(low, cols - d, 1), pltpu.roll(high_part, cols - d, 1)
-                )
-            shifted[d, pl.ds(r, fields, stride=high), :] = value
+        spare = jnp.zeros((pitch - fields, cols), jnp.float32)
+        at = pl.ds(pl.multiple_of(r * pitch, pitch), pitch)
+        for n in range(2):
+            value = jnp.where(keep, jnp.where(early, turned[n], turned[n + 1]), 0.0)
+            source[at, n * cols : (n + 1) * cols] = jnp.concatenate([value, spare], axis=0).astype(source.dtype)
         return 0
 
     lax.fori_loop(0, high, turn, 0)
-    wide = 2 * RIM + 1
-    for k in range(levels):
-        for b in range(rows // SUB):
-            near = slice(b * SUB, (b + 1) * SUB)
-            growi = lax.broadcasted_iota(jnp.int32, (SUB, cols), 0) + (lat * rows + b * SUB)
-            gpos = growi.astype(jnp.float32)
-            zdep = jnp.clip(float(k) - d_ref[k, near], 0.0, levels - 1.0)
-            ydep = jnp.clip(gpos - d_ref[levels + k, near], 0.0, total_rows - 1.0)
-            xrel = -d_ref[2 * levels + k, near]
-            zb = jnp.floor(zdep)
-            yb = jnp.floor(ydep)
-            xb = jnp.floor(xrel)
-            wz = spread(zb - 1.0, cubic_weights(zdep - zb), 0, levels - 1)
-            wy = spread(yb - gpos - 1.0, cubic_weights(ydep - yb), -RIM, RIM)
-            wx = spread(xb - 1.0, cubic_weights(xrel - xb), -RIM, RIM)
-
-            def tracer(t, _):
-                total = None
-                for z in range(levels):
-                    base = pl.multiple_of((t * levels + z) * high + b * SUB, SUB)
-                    plane = None
-                    for y in range(wide):
-                        line = None
-                        for x in range(wide):
-                            term = wx[x] * shifted[x, pl.ds(base + y, SUB), :]
-                            line = term if line is None else line + term
-                        term = wy[y] * line
-                        plane = term if plane is None else plane + term
-                    term = wz[z] * plane
-                    total = term if total is None else total + term
-                result[t * levels + k, near] = total
-                return 0
-
-            lax.fori_loop(0, ntrac, tracer, 0)
-    o_ref[...] = result[...].astype(o_ref.dtype)
+    tail = jnp.zeros((2 * cols - blocks * turn_rows, 2 * cols), source.dtype)
+
+    def row(i, _):
+        near = source[pl.ds(pl.multiple_of(i * pitch, pitch), wide * pitch), :]
+        for k in range(levels):
+            turned = wxs[k, pl.ds(i, turn_rows, stride=rows), :]
+            bit = 1
+            while bit < turn_rows:
+                turned = jnp.where((col_at & bit) != 0, pltpu.roll(turned, bit, 0), turned)
+                bit *= 2
+            head = turned.astype(source.dtype)
+            rest = (turned - head.astype(jnp.float32)).astype(source.dtype)
+            matrix = jnp.concatenate(
+                [jnp.concatenate([head * band[m], rest * band[m]], axis=1) for m in range(blocks)] + [tail],
+                axis=0,
+            )
+            lines = jnp.dot(near, matrix, preferred_element_type=jnp.float32)
+            total = None
+            for y in range(wide):
+                line = lines[y * pitch : y * pitch + fields]
+                term = wys[k * wide + y, pl.ds(i, 1), :] * (line[:, :cols] + line[:, cols:])
+                total = term if total is None else total + term
+            partial_sum[k] = total
+            value = None
+            for z in range(levels):
+                term = wzs[k * levels + z, pl.ds(i, 1), :] * partial_sum[k, pl.ds(z, ntrac, stride=levels), :]
+                value = term if value is None else value + term
+            result[pl.ds(k * rows + i, ntrac, stride=levels * rows), :] = value
+        return 0
+
+    lax.fori_loop(0, rows, row, 0)
+    o_ref[...] = result[...].reshape(o_ref.shape).astype(o_ref.dtype)
 
 
 def local(tracers, winds, zonal_shift):
@@ -315,6 +331,8 @@
     any_space = pl.BlockSpec(memory_space=pl.ANY)
     by_row = jnp.transpose(tracers.reshape(fields, rows, cols), (1, 0, 2))
     pieces = rows // RIM
+    band = 16
+    pitch = (fields + band - 1) // band * band
     gathered, shifts, disp = pl.pallas_call(
         functools.partial(exchange_kernel, nlat, nlon, levels),
         out_shape=(
@@ -344,8 +362,13 @@
         out_specs=vmem,
         scratch_shapes=[
             pltpu.VMEM((high, 3, fields, cols), tracers.dtype),
-            pltpu.VMEM((2 * RIM + 1, fields * high, cols), jnp.float32),
-            pltpu.VMEM((fields, rows, cols), jnp.float32),
+            pltpu.VMEM((high * pitch, 2 * cols), jnp.bfloat16),
+            pltpu.VMEM(((cols + 2 * RIM + band - 1) // band, band, cols), jnp.bfloat16),
+            pltpu.VMEM((levels, band * rows, cols), jnp.float32),
+            pltpu.VMEM(((2 * RIM + 1) * levels, rows, cols), jnp.float32),
+            pltpu.VMEM((levels * levels, rows, cols), jnp.float32),
+            pltpu.VMEM((levels, fields, cols), jnp.float32),
+            pltpu.VMEM((fields * rows, cols), jnp.float32),
             dma((high,)),
         ],
         name="stencil",

time: 53.1 us -> 44.9 us (0.85)
  Pallas kernels: 50 us -> 41.8 us
    pallas_call x1, Pallas kernels: 19.9 us -> 11.7 us  [local(): pl.pallas_call(functools.partial(stencil_kernel, nlat, nlon, levels, rows...]
where the time goes in v3:
time: 44.9 us; the launch traced here: 44.7 us
  Pallas kernels  41.8 us (93%)
  local copies, waits for them, and re-layouts  2.29 us (5%)
  between operations  0.66 us (1%)
    pallas_call x1, Pallas kernels, local(): pl.pallas_call(functools.partial(exchange_kernel, nlat, nlon, levels), ou...  30 us
    pallas_call x1, Pallas kernels, local(): pl.pallas_call(functools.partial(stencil_kernel, nlat, nlon, levels, rows...  11.7 us
    unnamed x4, local copies, waits for them, and re-layouts  2.29 us

profile of v3, /device:TPU:0, one launch (start us, length us, event | category | flops | bytes accessed | tf_op | source)
XLA Modules:
  0.0 44.7 jit_solution(17798654906049118683)
XLA Ops:
  0.6 1.6 %copy.5 = bf16[10,4,16,128]{3,1,0,2:T(4,128)(2,1)} copy(bf16[10,4,16,128]{3,2,1,0:T(8,128)(2,1)} %param.3) | data formatting | bytes 327680 | tf_op args[0]
  2.3 30.0 %exchange.1 = (bf16[8,24,40,128]{3,2,1,0:T(8,128)(2,1)}, s32[24,1,128]{2,1,0:T(1,128)}, f32[12,16,128]{2,1,0:T(8,128)}) custom-call(bf16[16,40,128]{2,1,0:T(8,128)(2,1)} %bitcast.6, f32[12,16,128]{2,1,0:T(8,128)} %bitcast.9, s32[16]{0:T(128)} %s_ref.1), custom_call_target="tpu_custom_call" | custom-call | tf_op jit(solution)/shard_map/exchange/pallas_call | solution.py:336
  32.3 0.0 copy-start
  32.3 11.7 %stencil.1 = bf16[40,16,128]{2,1,0:T(8,128)(2,1)} custom-call(s32[24,1,128]{2,1,0:T(1,128)} %get-tuple-element.5.s_ref, f32[12,16,128]{2,1,0:T(8,128)} %get-tuple-element.6.d_ref, bf16[8,24,40,128]{3,2,1,0:T(8,128)(2,1)} %get-tuple-element.7.g_ref), custom_call_target="tpu_custom_call" | custom-call | tf_op jit(solution)/shard_map/stencil/pallas_call | solution.py:358
  44.0 0.0 copy-done
  44.1 0.6 %copy.7 = f32[3,4,16,128]{3,2,1,0:T(8,128)} copy(f32[3,4,16,128]{3,2,1,0:T(8,128)S(1)} %bitcast.7) | data formatting | bytes 196608
Async XLA Ops:
  32.3 11.7 %copy-start = (f32[12,16,128]{2,1,0:T(8,128)S(1)}, f32[12,16,128]{2,1,0:T(8,128)}, u32[]{:S(2)}) copy-start(f32[12,16,128]{2,1,0:T(8,128)} %get-tuple-element.6.d_ref) | copy-start | bytes 294916

commit v4 on v3

--- a/solution.py
+++ b/solution.py
@@ -222,7 +222,7 @@
             ).wait_recv()
 
 
-def stencil_kernel(nlat, nlon, levels, rows, s_ref, d_ref, g_ref, o_ref, window, source, band, wxs, wys, wzs, partial_sum, result, sems):
+def stencil_kernel(nlat, nlon, levels, rows, s_ref, d_ref, g_ref, o_ref, d_out, window, source, band, wxs, wys, wzs, partial_sum, result, sems):
     high, fields, cols = g_ref.shape[1:]
     ntrac = fields // levels
     pitch = source.shape[0] // high
@@ -244,6 +244,7 @@
 
     lax.fori_loop(0, high, start, 0)
 
+    d_out[...] = d_ref[...]
     gpos = (lax.broadcasted_iota(jnp.int32, (rows, cols), 0) + lat * rows).astype(jnp.float32)
     for k in range(levels):
         zdep = jnp.clip(float(k) - d_ref[k], 0.0, levels - 1.0)
@@ -284,7 +285,7 @@
             source[at, n * cols : (n + 1) * cols] = jnp.concatenate([value, spare], axis=0).astype(source.dtype)
         return 0
 
-    lax.fori_loop(0, high, turn, 0)
+    lax.fori_loop(0, high, turn, 0, unroll=4)
     tail = jnp.zeros((2 * cols - blocks * turn_rows, 2 * cols), source.dtype)
 
     def row(i, _):
@@ -315,7 +316,7 @@
             result[pl.ds(k * rows + i, ntrac, stride=levels * rows), :] = value
         return 0
 
-    lax.fori_loop(0, rows, row, 0)
+    lax.fori_loop(0, rows, row, 0, unroll=2)
     o_ref[...] = result[...].reshape(o_ref.shape).astype(o_ref.dtype)
 
 
@@ -355,11 +356,14 @@
         compiler_params=pltpu.CompilerParams(collective_id=0, has_side_effects=True),
         name="exchange",
     )(by_row, winds.reshape(planes, rows, cols), zonal_shift)
-    out = pl.pallas_call(
+    out, disp = pl.pallas_call(
         functools.partial(stencil_kernel, nlat, nlon, levels, rows),
-        out_shape=jax.ShapeDtypeStruct((fields, rows, cols), tracers.dtype),
+        out_shape=(
+            jax.ShapeDtypeStruct((fields, rows, cols), tracers.dtype),
+            jax.ShapeDtypeStruct((planes, rows, cols), jnp.float32),
+        ),
         in_specs=[pl.BlockSpec(memory_space=pltpu.SMEM), vmem, any_space],
-        out_specs=vmem,
+        out_specs=(vmem, vmem),
         scratch_shapes=[
             pltpu.VMEM((high, 3, fields, cols), tracers.dtype),
             pltpu.VMEM((high * pitch, 2 * cols), jnp.bfloat16),

time: 44.9 us -> 42.7 us (0.951)
  Pallas kernels: 41.8 us -> 40.2 us
  local copies, waits for them, and re-layouts: 2.29 us -> 1.65 us
    pallas_call x1, Pallas kernels: 11.7 us -> 10.2 us  [local(): pl.pallas_call(functools.partial(stencil_kernel, nlat, nlon, levels, rows...]
    unnamed x4 -> x1, local copies, waits for them, and re-layouts: 2.29 us -> 1.65 us
where the time goes in v4:
time: 42.7 us; the launch traced here: 42.5 us
  Pallas kernels  40.2 us (94%)
  local copies, waits for them, and re-layouts  1.65 us (4%)
  between operations  0.64 us (1%)
    pallas_call x1, Pallas kernels, local(): pl.pallas_call(functools.partial(exchange_kernel, nlat, nlon, levels), ou...  30 us
    pallas_call x1, Pallas kernels, local(): pl.pallas_call(functools.partial(stencil_kernel, nlat, nlon, levels, rows...  10.2 us
    unnamed x1, local copies, waits for them, and re-layouts  1.65 us

profile of v4, /device:TPU:0, one launch (start us, length us, event | category | flops | bytes accessed | tf_op | source)
XLA Modules:
  0.0 42.5 jit_solution(2131498631812804515)
XLA Ops:
  0.6 1.6 %copy.5 = bf16[10,4,16,128]{3,1,0,2:T(4,128)(2,1)} copy(bf16[10,4,16,128]{3,2,1,0:T(8,128)(2,1)} %param.3) | data formatting | bytes 327680 | tf_op args[0]
  2.3 30.0 %exchange.1 = (bf16[8,24,40,128]{3,2,1,0:T(8,128)(2,1)}, s32[24,1,128]{2,1,0:T(1,128)}, f32[12,16,128]{2,1,0:T(8,128)}) custom-call(bf16[16,40,128]{2,1,0:T(8,128)(2,1)} %bitcast.6, f32[12,16,128]{2,1,0:T(8,128)} %bitcast.7, s32[16]{0:T(128)} %s_ref.1), custom_call_target="tpu_custom_call" | custom-call | tf_op jit(solution)/shard_map/exchange/pallas_call | solution.py:337
  32.3 10.2 %stencil.1 = (bf16[40,16,128]{2,1,0:T(8,128)(2,1)}, f32[12,16,128]{2,1,0:T(8,128)}) custom-call(s32[24,1,128]{2,1,0:T(1,128)} %get-tuple-element.7.s_ref, f32[12,16,128]{2,1,0:T(8,128)} %get-tuple-element.8.d_ref, bf16[8,24,40,128]{3,2,1,0:T(8,128)(2,1)} %get-tuple-element.9.g_ref), custom_call_target="tpu_custom_call" | custom-call | tf_op jit(solution)/shard_map/stencil/pallas_call | solution.py:359
